TPU v7x, 256 devices: a whole 4x4x8 slice. The times are simulated.
256 devices in a mesh: tm: 16 (over z, x_lo), lon: 4 (over x_hi, core), lat: 4 (over y).
Axes of the slice: x: 4 (x_hi: 2, x_lo: 2; x = x_hi * 2 + x_lo), y: 4, z: 8, core: 2. Of those that a mesh axis runs over, the one named last changes fastest.
Arguments:
- iterate: float32 [16, 64, 64, 512], P('tm', None, 'lat', 'lon'), may hold values from -6 to 6
- heating: float32 [16, 64, 64, 512], P('tm', None, 'lat', 'lon'), may hold values from -6 to 6
- initial: float32 [64, 64, 512], P(None, 'lat', 'lon'), may hold values from -6 to 6
- region: int32 [64, 64, 512], P(None, 'lat', 'lon'), may hold values from 0 to 7
- cond_table: float32 [8], replicated, may hold values from 0.3 to 3
Outputs:
- updated: float32 [16, 64, 64, 512], P('tm', None, 'lat', 'lon')
Inputs may be any that keep to these rules, and one draw needn't show every extreme that they name: `region`: class index of each cell.
All inputs are finite; a program needn't handle non-finite values.
Results may differ from a plain program's by a relative error of at most 0.0003.
Values sent between devices are 32-bit elements; how exact they have to be, the bound alone decides.
A program may use at most 128 MiB of HBM per device.

v0:
```python
import jax
import jax.numpy as jnp
from jax import lax
from jax.sharding import PartitionSpec as P

SWEEPS = 4
corner_weight = 0.1


def padded(value, sides, width, wrap):
    for axis, dim in sides:
        peers, length = (lax.axis_size(axis), value.shape[dim])
        up = [(i, (i + 1) % peers) for i in range(peers if wrap else peers - 1)]
        down = [(j, i) for i, j in up]
        last = lax.slice_in_dim(value, length - width, length, axis=dim)
        initial = lax.slice_in_dim(value, 0, width, axis=dim)
        before = lax.ppermute(last, axis, up)
        after = lax.ppermute(initial, axis, down)
        value = jnp.concatenate([before, value, after], axis=dim)
    return value


def passed_along(block, axis, distance):
    devices = range(lax.axis_size(axis))
    route = [(i - distance, i) for i in devices if i - distance in devices]
    return lax.ppermute(block, axis, route)


def harmonic(first, second):
    return 2.0 * first * second / (first + second)


def conductivity(region, cond_table):
    classes = jnp.arange(cond_table.shape[0], dtype=jnp.int32)
    onehot = (region[..., None] == classes).astype(jnp.float32)
    return jnp.sum(onehot * cond_table, axis=-1)


def extend(stack):
    lat_ext = padded(stack, (("lat", 2),), 1, False)
    both = padded(lat_ext, (("lon", 3),), 1, True)
    return jnp.pad(both, ((0, 0), (1, 1), (0, 0), (0, 0)))


def face_weights(kext):
    centre = kext[1:-1, 1:-1, 1:-1]
    return (
        harmonic(centre, kext[:-2, 1:-1, 1:-1]),
        harmonic(centre, kext[2:, 1:-1, 1:-1]),
        harmonic(centre, kext[1:-1, :-2, 1:-1]),
        harmonic(centre, kext[1:-1, 2:, 1:-1]),
        harmonic(centre, kext[1:-1, 1:-1, :-2]),
        harmonic(centre, kext[1:-1, 1:-1, 2:]),
    )


def neighbours(weights, ext):
    near = weights[0] * ext[..., :-2, 1:-1, 1:-1] + weights[1] * ext[..., 2:, 1:-1, 1:-1]
    near = near + weights[2] * ext[..., 1:-1, :-2, 1:-1] + weights[3] * ext[..., 1:-1, 2:, 1:-1]
    near = near + weights[4] * ext[..., 1:-1, 1:-1, :-2] + weights[5] * ext[..., 1:-1, 1:-1, 2:]
    return near


def on_device(iterate, heating, initial, region, cond_table):
    steps = lax.axis_size("tm")
    own = lax.axis_index("tm")
    high = lax.Precision.HIGHEST
    kfield = conductivity(region, cond_table)
    ext = extend(jnp.stack([kfield, iterate[0]]))
    weights = face_weights(ext[0])
    total = weights[0] + weights[1] + weights[2] + weights[3] + weights[4] + weights[5]
    shifted = passed_along(iterate, "tm", 1)[0]
    previous = jnp.where(own == 0, initial, shifted)
    residual = heating[0] + previous - ((1.0 + total) * iterate[0] - neighbours(weights, ext[1]))
    scale_own = corner_weight ** (own.astype(jnp.float32) / steps)
    scaled = residual * scale_own
    zeros = jnp.zeros_like(residual)
    piece = lax.all_gather(scaled[None], "tm", axis=0, tiled=True)
    order = jnp.arange(piece.shape[0], dtype=jnp.int32)
    angle = 2.0 * jnp.pi / steps * (own * order % steps).astype(jnp.float32)
    real_part = jnp.einsum("n,nabc->abc", jnp.cos(angle), piece, precision=high)
    imag_part = (zeros, zeros)[1] - jnp.einsum("n,nabc->abc", jnp.sin(angle), piece, precision=high)
    beta = corner_weight ** (1.0 / steps)
    freq_angle = 2.0 * jnp.pi / steps * (own % steps).astype(jnp.float32)
    diag_re = 1.0 - beta * jnp.cos(freq_angle) + total
    diag_im = beta * jnp.sin(freq_angle) + zeros
    denom = diag_re * diag_re + diag_im * diag_im
    inv_re = diag_re / denom
    inv_im = -diag_im / denom
    sol_re = real_part * inv_re - imag_part * inv_im
    sol_im = real_part * inv_im + imag_part * inv_re
    for sweep in range(SWEEPS - 1):
        near = neighbours(weights, extend(jnp.stack([sol_re, sol_im])))
        rhs_re = real_part + near[0]
        rhs_im = imag_part + near[1]
        sol_re = rhs_re * inv_re - rhs_im * inv_im
        sol_im = rhs_re * inv_im + rhs_im * inv_re
    pieces = (
        lax.all_gather(sol_re[None], "tm", axis=0, tiled=True),
        lax.all_gather(sol_im[None], "tm", axis=0, tiled=True),
    )
    order = jnp.arange(pieces[0].shape[0], dtype=jnp.int32)
    angle = 2.0 * jnp.pi / steps * (order * own % steps).astype(jnp.float32)
    summed = jnp.einsum("k,kabc->abc", jnp.cos(angle), pieces[0], precision=high) - jnp.einsum(
        "k,kabc->abc", jnp.sin(angle), pieces[1], precision=high
    )
    back = summed / steps
    return iterate + (back / scale_own)[None]


def solution(mesh):
    return jax.shard_map(
        on_device,
        mesh=mesh,
        in_specs=(
            P("tm", None, "lat", "lon"),
            P("tm", None, "lat", "lon"),
            P(None, "lat", "lon"),
            P(None, "lat", "lon"),
            P(),
        ),
        out_specs=P("tm", None, "lat", "lon"),
        check_vma=False,
    )
```

profile of v0, /device:TPU:34, one launch (start us, length us, event | category | flops | bytes accessed | tf_op | source)
XLA Modules:
  0.0 730.6 jit_solution(5126643289084944055)
XLA Ops:
  10.2 3.5 collective-permute-start.1
  15.5 4.3 collective-permute-done.2
  25.1 3.3 collective-permute-start.4
  28.4 3.8 collective-permute-start
  34.6 4.0 select_maximum_fusion.15
  38.9 4.6 collective-permute-done
  43.5 3.9 fusion.45
  47.8 190.2 %all-gather.7.cloned.1.call-done = f32[1024,16,128]{2,1,0:T(8,128)} async-done(((f32[64,16,128]{2,1,0:T(8,128)}), f32[1024,16,128]{2,1,0:T(8,128)}) %all-gather.7.cloned.1.call-update) | async-done | bytes 8388624 | tf_op jit(solution)/shard_map/all_gather | solution.py:78
  238.0 12.6 %fusion.4 = f32[1,64,16,128]{3,0,2,1:T(1,128)S(1)} fusion(f32[16,64,16,128]{3,2,1,0:T(8,128)} %bitcast.108, s32[]{:T(128)S(6)} %axis_index.15), kind=kOutput, calls=%fused_computation.4 | convolution fusion | flops 25166048 | bytes 8912900 | tf_op jit(solution)/shard_map/n,nabc->abc/dot_general | solution.py:82
  250.6 7.8 %fusion.6 = f32[1,64,16,128]{3,0,2,1:T(1,128)S(1)} fusion(f32[16,64,16,128]{3,2,1,0:T(8,128)S(1)} %bitcast.109, s32[]{:T(128)S(6)} %axis_index.15), kind=kOutput, calls=%fused_computation.6 | convolution fusion | flops 25166048 | bytes 8912900 | tf_op jit(solution)/shard_map/n,nabc->abc/dot_general | solution.py:81
  259.1 3.4 collective-permute-start.5
  264.4 4.3 collective-permute-done.6
  273.1 3.3 collective-permute-start.8
  279.7 4.3 select_maximum_fusion.10
  286.9 3.4 collective-permute-start.9
  292.2 4.3 collective-permute-done.10
  307.3 4.3 select_maximum_fusion.5
  314.5 3.5 collective-permute-start.13
  319.9 4.3 collective-permute-done.14
  335.1 4.3 select_maximum_fusion
  343.9 181.1 %all-gather.11.cloned.1.call-done = f32[1024,16,128]{2,1,0:T(8,128)} async-done(((f32[64,16,128]{2,1,0:T(8,128)}), f32[1024,16,128]{2,1,0:T(8,128)}) %all-gather.11.cloned.1.call-update) | async-done | bytes 8388624 | tf_op jit(solution)/shard_map/all_gather | solution.py:100
  525.0 12.4 %fusion = f32[1,64,16,128]{3,0,2,1:T(1,128)S(1)} fusion(f32[16,64,16,128]{3,2,1,0:T(8,128)} %bitcast.120, s32[]{:T(128)S(6)} %axis_index.15), kind=kOutput, calls=%fused_computation | convolution fusion | flops 25166048 | bytes 8912900 | tf_op jit(solution)/shard_map/k,kabc->abc/dot_general | solution.py:104
  537.5 173.0 %all-gather.9.cloned.1.call-done = f32[1024,16,128]{2,1,0:T(8,128)} async-done(((f32[64,16,128]{2,1,0:T(8,128)}), f32[1024,16,128]{2,1,0:T(8,128)}) %all-gather.9.cloned.1.call-update) | async-done | bytes 8388624 | tf_op jit(solution)/shard_map/all_gather | solution.py:99
  710.5 12.5 %fusion.2 = f32[1,64,16,128]{3,0,2,1:T(1,128)S(1)} fusion(f32[16,64,16,128]{3,2,1,0:T(8,128)} %bitcast.121, s32[]{:T(128)S(6)} %axis_index.15), kind=kOutput, calls=%fused_computation.2 | convolution fusion | flops 25166048 | bytes 8912900 | tf_op jit(solution)/shard_map/k,kabc->abc/dot_general | solution.py:104
  (155 shorter events, 59.9 us)
Async XLA Ops:
  6.5 231.4 %all-gather.7.cloned.1.call-start = ((), (), s32[]{:S(2)}) async-start(), calls=%async_computation | async-start | bytes 8912896 | tf_op jit(solution)/shard_map/all_gather | solution.py:78
  10.2 5.4 collective-permute-start.1
  13.7 6.2 collective-permute-start.2
  24.6 7.7 %collective-permute-start.3 = (f32[2,64,18,1]{1,0,3,2:T(2,128)S(1)}, f32[2,64,18,1]{1,0,3,2:T(2,128)S(1)}, u32[]{:S(2)}, u32[]{:S(2)}) collective-permute-start(f32[2,64,18,1]{1,0,3,2:T(2,128)S(1)} %copy.57), channel_id=1, source_target_pairs={{0,4},{4,8},{8,12},{12,0},{1,5},{5,9},{9,13},{13,1},{2,6},{6,10},{... | collective-permute-start | bytes 27656 | tf_op jit(solution)/shard_map/ppermute | solution.py:17
  25.1 7.7 %collective-permute-start.4 = (f32[2,64,18,1]{1,0,3,2:T(2,128)S(1)}, f32[2,64,18,1]{1,0,3,2:T(2,128)S(1)}, u32[]{:S(2)}, u32[]{:S(2)}) collective-permute-start(f32[2,64,18,1]{1,0,3,2:T(2,128)S(1)} %copy.58), channel_id=1, source_target_pairs={{4,0},{8,4},{12,8},{0,12},{5,1},{9,5},{13,9},{1,13},{6,2},{10,6},{... | collective-permute-start | bytes 27656 | tf_op jit(solution)/shard_map/ppermute | solution.py:18
  28.4 15.0 %collective-permute-start = (f32[1,64,16,128]{3,2,1,0:T(8,128)S(1)}, f32[1,64,16,128]{3,2,1,0:T(8,128)}, u32[]{:S(2)}, u32[]{:S(2)}) collective-permute-start(f32[1,64,16,128]{3,2,1,0:T(8,128)S(1)} %copy-done.4), channel_id=1, source_target_pairs={{0,16},{16,32},{32,48},{48,64},{64,80},{80,96},{96,112},{112,128},... | collective-permute-start | bytes 1572872 | tf_op jit(solution)/shard_map/ppermute | solution.py:26
  47.4 211.1 %copy-start.18 = (f32[64,16,128]{2,1,0:T(8,128)}, f32[64,16,128]{2,1,0:T(8,128)S(1)}, u32[]{:S(2)}) copy-start(f32[64,16,128]{2,1,0:T(8,128)S(1)} %get-tuple-element.8) | copy-start | bytes 1572868
  47.4 211.1 %copy-start.22 = (f32[64,16,128]{2,1,0:T(8,128)}, f32[64,16,128]{2,1,0:T(8,128)S(1)}, u32[]{:S(2)}) copy-start(f32[64,16,128]{2,1,0:T(8,128)S(1)} %get-tuple-element.9) | copy-start | bytes 1572868
  47.4 211.1 %copy-start.26 = (f32[64,16,128]{2,1,0:T(8,128)}, f32[64,16,128]{2,1,0:T(8,128)S(1)}, u32[]{:S(2)}) copy-start(f32[64,16,128]{2,1,0:T(8,128)S(1)} %get-tuple-element.10) | copy-start | bytes 1572868
  47.4 477.6 %all-gather.11.cloned.1.call-start = ((), (), s32[]{:S(2)}) async-start(), calls=%async_computation.2 | async-start | bytes 8912896 | tf_op jit(solution)/shard_map/all_gather | solution.py:100
  238.0 12.6 %copy-start = (f32[1024,16,128]{2,1,0:T(8,128)S(1)}, f32[1024,16,128]{2,1,0:T(8,128)}, u32[]{:S(2)}) copy-start(f32[1024,16,128]{2,1,0:T(8,128)} %all-gather.7.cloned.1.call-done) | copy-start | bytes 25165828
  259.1 5.3 collective-permute-start.5
  262.5 6.2 collective-permute-start.6
  272.4 5.0 collective-permute-start.7
  273.1 4.8 collective-permute-start.8
  286.9 5.3 collective-permute-start.9
  290.3 6.2 collective-permute-start.10
  300.2 4.8 collective-permute-start.11
  301.4 4.1 collective-permute-start.12
  314.5 5.4 collective-permute-start.13
  318.0 6.2 collective-permute-start.14
  327.9 4.8 collective-permute-start.15
  329.6 3.7 collective-permute-start.16
  343.1 367.4 %all-gather.9.cloned.1.call-start = ((), (), s32[]{:S(2)}) async-start(), calls=%async_computation.1 | async-start | bytes 8912896 | tf_op jit(solution)/shard_map/all_gather | solution.py:99
  (40 other events, 230.7 us)
Sparse Core Ops, SparseCore 0:
  47.5 190.4 all-gather.6
  343.3 181.7 all-gather.10
  526.8 183.6 all-gather.8
where the time goes:
time: 738 us; the launch traced here: 731 us
  waiting for transfers between devices  572 us (78%)
  matrix products  45.4 us (6%)
  other arithmetic  37.1 us (5%)
  starting transfers between devices  36.8 us (5%)
  local copies, waits for them, and re-layouts  25.3 us (3%)
  between operations  14.4 us (2%)
    all_gather x1, waiting for transfers between devices, on_device(): piece = lax.all_gather(scaled[None], 'tm', axis=0, tiled=True)  190 us
    all_gather x1, waiting for transfers between devices, on_device(): lax.all_gather(sol_im[None], 'tm', axis=0, tiled=True)  181 us
    all_gather x1, waiting for transfers between devices, on_device(): lax.all_gather(sol_re[None], 'tm', axis=0, tiled=True)  173 us
    concatenate x8, other arithmetic, padded(): value = jnp.concatenate([before, value, after], axis=dim)  19 us
    ppermute x8, waiting for transfers between devices, padded(): after = lax.ppermute(initial, axis, down)  17.1 us
    ppermute x8, starting transfers between devices, padded(): after = lax.ppermute(initial, axis, down)  16.5 us
    ppermute x8, starting transfers between devices, padded(): before = lax.ppermute(last, axis, up)  16.1 us
  transfers between devices with their start and end apart: 20, of which 15 were waited for; matrix products, arithmetic and copies ran while one was open for 3% of the time, Pallas kernels for 0%

commit v1 on v0

--- a/solution.py
+++ b/solution.py
@@ -5,6 +5,15 @@
 
 SWEEPS = 4
 corner_weight = 0.1
+
+
+def detail_the_files(local_block, axis_name, in_dim):
+    return jnp.concatenate(
+        lax.all_to_all(
+            jnp.stack([local_block for _ in range(lax.axis_size(axis_name))]), axis_name, 0, 0
+        ),
+        axis=in_dim,
+    )
 
 
 def padded(value, sides, width, wrap):
@@ -96,7 +105,7 @@
         sol_re = rhs_re * inv_re - rhs_im * inv_im
         sol_im = rhs_re * inv_im + rhs_im * inv_re
     pieces = (
-        lax.all_gather(sol_re[None], "tm", axis=0, tiled=True),
+        detail_the_files(sol_re[None], "tm", 0),
         lax.all_gather(sol_im[None], "tm", axis=0, tiled=True),
     )
     order = jnp.arange(pieces[0].shape[0], dtype=jnp.int32)

time: 738 us -> 708 us (0.959)
  waiting for transfers between devices: 572 us -> 520 us
  local copies, waits for them, and re-layouts: 25.3 us -> 35.1 us
    all_gather x1 -> x0, waiting for transfers between devices: 173 us -> none  [on_device(): lax.all_gather(sol_re[None], 'tm', axis=0, tiled=True)]
    all_gather x1, waiting for transfers between devices: 181 us -> 304 us  [on_device(): lax.all_gather(sol_im[None], 'tm', axis=0, tiled=True)]
  transfers between devices with their start and end apart: 20 -> 20, of which waited for: 15 -> 14; matrix products, arithmetic and copies ran while one was open for 3% -> 4% of each run, Pallas kernels for 0% -> 0%
where the time goes in v1:
time: 708 us; the launch traced here: 695 us
  waiting for transfers between devices  520 us (73%)
  matrix products  45.4 us (6%)
  starting transfers between devices  43.3 us (6%)
  other arithmetic  36 us (5%)
  local copies, waits for them, and re-layouts  35.1 us (5%)
  between operations  14.7 us (2%)
    all_gather x1, waiting for transfers between devices, on_device(): lax.all_gather(sol_im[None], 'tm', axis=0, tiled=True)  304 us
    all_gather x1, waiting for transfers between devices, on_device(): piece = lax.all_gather(scaled[None], 'tm', axis=0, tiled=True)  190 us
    ppermute x8, waiting for transfers between devices, padded(): after = lax.ppermute(initial, axis, down)  19.7 us
    concatenate x8, other arithmetic, padded(): value = jnp.concatenate([before, value, after], axis=dim)  19 us
    ppermute x8, starting transfers between devices, padded(): after = lax.ppermute(initial, axis, down)  16.9 us
    ppermute x8, starting transfers between devices, padded(): before = lax.ppermute(last, axis, up)  15.7 us
    slice x8, local copies, waits for them, and re-layouts, padded(): last = lax.slice_in_dim(value, length - width, length, axis=dim)  15.4 us
  transfers between devices with their start and end apart: 20, of which 14 were waited for; matrix products, arithmetic and copies ran while one was open for 4% of the time, Pallas kernels for 0%

profile of v1, /device:TPU:34, one launch (start us, length us, event | category | flops | bytes accessed | tf_op | source)
XLA Modules:
  0.0 694.6 jit_solution(13261720924664742175)
XLA Ops:
  10.2 3.5 collective-permute-start.1
  15.5 4.3 collective-permute-done.2
  25.1 3.3 collective-permute-start.4
  28.4 3.8 collective-permute-start
  34.6 4.0 select_maximum_fusion.15
  38.9 4.6 collective-permute-done
  46.9 190.2 %all-gather.5.cloned.1.call-done = f32[1024,16,128]{2,1,0:T(8,128)} async-done(((f32[64,16,128]{2,1,0:T(8,128)}), f32[1024,16,128]{2,1,0:T(8,128)}) %all-gather.5.cloned.1.call-update) | async-done | bytes 8388624 | tf_op jit(solution)/shard_map/all_gather | solution.py:87
  237.2 12.6 %fusion.4 = f32[1,64,16,128]{3,0,2,1:T(1,128)S(1)} fusion(f32[16,64,16,128]{3,2,1,0:T(8,128)} %bitcast.108, s32[]{:T(128)S(6)} %axis_index.15), kind=kOutput, calls=%fused_computation.4 | convolution fusion | flops 25166048 | bytes 8912900 | tf_op jit(solution)/shard_map/n,nabc->abc/dot_general | solution.py:91
  249.8 7.8 %fusion.6 = f32[1,64,16,128]{3,0,2,1:T(1,128)S(1)} fusion(f32[16,64,16,128]{3,2,1,0:T(8,128)S(1)} %bitcast.109, s32[]{:T(128)S(6)} %axis_index.15), kind=kOutput, calls=%fused_computation.6 | convolution fusion | flops 25166048 | bytes 8912900 | tf_op jit(solution)/shard_map/n,nabc->abc/dot_general | solution.py:90
  258.3 3.4 collective-permute-start.5
  263.6 4.3 collective-permute-done.6
  274.2 3.3 collective-permute-start.8
  280.7 4.3 select_maximum_fusion.10
  287.9 3.4 collective-permute-start.9
  293.2 4.3 collective-permute-done.10
  310.1 4.3 select_maximum_fusion.5
  317.3 3.1 collective-permute-start.13
  322.3 4.3 collective-permute-done.14
  339.2 4.3 select_maximum_fusion
  347.1 4.1 stack.47
  351.3 6.7 all-to-all-start
  357.9 303.8 %all-gather.7.cloned.1.call-done = f32[1024,16,128]{2,1,0:T(8,128)} async-done(((f32[64,16,128]{2,1,0:T(8,128)}), f32[1024,16,128]{2,1,0:T(8,128)}) %all-gather.7.cloned.1.call-update) | async-done | bytes 8388624 | tf_op jit(solution)/shard_map/all_gather | solution.py:109
  661.7 12.4 %fusion = f32[1,64,16,128]{3,0,2,1:T(1,128)S(1)} fusion(f32[16,64,16,128]{3,2,1,0:T(8,128)} %bitcast.120, s32[]{:T(128)S(6)} %axis_index.15), kind=kOutput, calls=%fused_computation | convolution fusion | flops 25166048 | bytes 8912900 | tf_op jit(solution)/shard_map/k,kabc->abc/dot_general | solution.py:113
  674.2 12.5 %fusion.2 = f32[1,64,16,128]{3,0,2,1:T(1,128)S(1)} fusion(f32[16,64,16,128]{3,2,1,0:T(8,128)} %bitcast.29, s32[]{:T(128)S(6)} %axis_index.15), kind=kOutput, calls=%fused_computation.2 | convolution fusion | flops 25166048 | bytes 8912900 | tf_op jit(solution)/shard_map/k,kabc->abc/dot_general | solution.py:113
  (155 shorter events, 67.4 us)
Async XLA Ops:
  6.5 230.6 %all-gather.5.cloned.1.call-start = ((), (), s32[]{:S(2)}) async-start(), calls=%async_computation.1 | async-start | bytes 8912896 | tf_op jit(solution)/shard_map/all_gather | solution.py:87
  10.2 5.4 collective-permute-start.1
  13.7 6.2 collective-permute-start.2
  24.6 7.7 %collective-permute-start.3 = (f32[2,64,18,1]{1,0,3,2:T(2,128)S(1)}, f32[2,64,18,1]{1,0,3,2:T(2,128)S(1)}, u32[]{:S(2)}, u32[]{:S(2)}) collective-permute-start(f32[2,64,18,1]{1,0,3,2:T(2,128)S(1)} %copy.57), channel_id=1, source_target_pairs={{0,4},{4,8},{8,12},{12,0},{1,5},{5,9},{9,13},{13,1},{2,6},{6,10},{... | collective-permute-start | bytes 27656 | tf_op jit(solution)/shard_map/ppermute | solution.py:26
  25.1 7.7 %collective-permute-start.4 = (f32[2,64,18,1]{1,0,3,2:T(2,128)S(1)}, f32[2,64,18,1]{1,0,3,2:T(2,128)S(1)}, u32[]{:S(2)}, u32[]{:S(2)}) collective-permute-start(f32[2,64,18,1]{1,0,3,2:T(2,128)S(1)} %copy.58), channel_id=1, source_target_pairs={{4,0},{8,4},{12,8},{0,12},{5,1},{9,5},{13,9},{1,13},{6,2},{10,6},{... | collective-permute-start | bytes 27656 | tf_op jit(solution)/shard_map/ppermute | solution.py:27
  28.4 15.0 %collective-permute-start = (f32[1,64,16,128]{3,2,1,0:T(8,128)S(1)}, f32[1,64,16,128]{3,2,1,0:T(8,128)S(1)}, u32[]{:S(2)}, u32[]{:S(2)}) collective-permute-start(f32[1,64,16,128]{3,2,1,0:T(8,128)S(1)} %copy-done.4), channel_id=1, source_target_pairs={{0,16},{16,32},{32,48},{48,64},{64,80},{80,96},{96,112},{112,128},... | collective-permute-start | bytes 1572872 | tf_op jit(solution)/shard_map/ppermute | solution.py:35
  46.5 211.1 %copy-start.18 = (f32[64,16,128]{2,1,0:T(8,128)}, f32[64,16,128]{2,1,0:T(8,128)S(1)}, u32[]{:S(2)}) copy-start(f32[64,16,128]{2,1,0:T(8,128)S(1)} %get-tuple-element.8) | copy-start | bytes 1572868
  46.5 211.1 %copy-start.22 = (f32[64,16,128]{2,1,0:T(8,128)}, f32[64,16,128]{2,1,0:T(8,128)S(1)}, u32[]{:S(2)}) copy-start(f32[64,16,128]{2,1,0:T(8,128)S(1)} %get-tuple-element.9) | copy-start | bytes 1572868
  46.6 615.2 %all-gather.7.cloned.1.call-start = ((), (), s32[]{:S(2)}) async-start(), calls=%async_computation.2 | async-start | bytes 8912896 | tf_op jit(solution)/shard_map/all_gather | solution.py:109
  237.2 12.6 %copy-start = (f32[1024,16,128]{2,1,0:T(8,128)S(1)}, f32[1024,16,128]{2,1,0:T(8,128)}, u32[]{:S(2)}) copy-start(f32[1024,16,128]{2,1,0:T(8,128)} %all-gather.5.cloned.1.call-done) | copy-start | bytes 25165828
  258.3 5.3 collective-permute-start.5
  261.7 6.2 collective-permute-start.6
  272.1 5.4 collective-permute-start.7
  274.2 4.8 collective-permute-start.8
  287.9 5.3 collective-permute-start.9
  291.3 6.2 collective-permute-start.10
  301.7 5.2 collective-permute-start.11
  304.3 4.0 collective-permute-start.12
  317.3 5.0 collective-permute-start.13
  320.4 6.2 collective-permute-start.14
  330.8 5.2 collective-permute-start.15
  333.9 3.6 collective-permute-start.16
  351.3 322.9 %all-to-all-start = ((f32[16,1,64,16,128]{4,3,2,1,0:T(8,128)}), f32[16,1,64,16,128]{4,3,2,1,0:T(8,128)}, u32[]{:S(2)}, u32[]{:S(2)}) async-start(f32[16,1,64,16,128]{4,3,2,1,0:T(8,128)} %stack.47), calls=%async_computation | async-start | bytes 16777216 | tf_op jit(solution)/shard_map/all_to_all | solution.py:12
  674.2 12.5 %copy-start.5 = (f32[1,64,16,128]{3,2,1,0:T(8,128)S(1)}, f32[1,64,16,128]{3,2,1,0:T(8,128)}, u32[]{:S(2)}) copy-start(f32[1,64,16,128]{3,2,1,0:T(8,128)} %param.5) | copy-start | bytes 1572868
  (40 other events, 239.6 us)
Sparse Core Ops, SparseCore 0:
  46.7 190.4 all-gather.4
  347.2 314.4 all-gather.6
